TPU v7x, 32 devices: a whole 2x2x4 slice. The times are simulated.
32 devices in a mesh: band: 8 (over z, x), cuts: 4 (over y, core).
Axes of the slice: x: 2, y: 2, z: 4, core: 2. Of those that a mesh axis runs over, the one named last changes fastest.
Arguments:
- var_feat: bfloat16 [163840, 128], P(('band', 'cuts')), may hold values from -6 to 6
- con_feat: bfloat16 [4096, 128], P(('band', 'cuts')), may hold values from -6 to 6
- slot_column_block: int32 [5120], P(('band', 'cuts')), may hold values from 0 to 39
- slot_constraint_block: int32 [5120], P(('band', 'cuts')), may hold values from 0 to 7
- block_count: int32 [32], P(('band', 'cuts')), may hold values from 40 to 160, as said below
- incidence_coefficients: int32 [5120, 128, 128], P(('band', 'cuts')), may hold values from -3 to 4
- con_first: bfloat16 [256, 256], replicated, may hold values from -0.375 to 0.375
- con_bias: float32 [256], replicated, may hold values from -3 to 3
- con_second: bfloat16 [256, 256], replicated, may hold values from -0.375 to 0.375
- con_third: bfloat16 [256, 128], replicated, may hold values from -0.375 to 0.375
- con_gain: float32 [128], replicated, may hold values from 0.1 to 1.9
- con_shift: float32 [128], replicated, may hold values from -3 to 3
- var_first: bfloat16 [256, 256], replicated, may hold values from -0.375 to 0.375
- var_bias: float32 [256], replicated, may hold values from -3 to 3
- var_second: bfloat16 [256, 256], replicated, may hold values from -0.375 to 0.375
- var_third: bfloat16 [256, 128], replicated, may hold values from -0.375 to 0.375
- var_gain: float32 [128], replicated, may hold values from 0.1 to 1.9
- var_shift: float32 [128], replicated, may hold values from -3 to 3
Outputs:
- con_new: bfloat16 [4096, 128], P(('band', 'cuts'))
- var_new: bfloat16 [163840, 128], P(('band', 'cuts'))
Inputs may be any that keep to these rules, and one draw needn't show every extreme that they name: Each device's live slots are its first block_count slots; in every draw one eighth of the devices hold 160 live slots and some device holds 40.
All inputs are finite; a program needn't handle non-finite values.
Results may differ from a plain program's by a relative error of at most 0.0075.
Values may be sent and summed in bfloat16 or wider, within the bound.
A program may use at most 128 MiB of HBM per device.

v0:
```python
import functools
import math

import jax
import jax.numpy as jnp
from jax import lax
from jax.experimental import pallas as pl
from jax.experimental.pallas import tpu as pltpu
from jax.sharding import PartitionSpec as P

EPS = 1e-05
F32 = jnp.float32
BF16 = jnp.bfloat16
MESH = pl.DeviceIdType.MESH
CHUNK = 16
UNROLL = 8
FORWARD = 22
BACK = 25
STEP = 10
GATHER = 8


def layer_norm(values, gain, offset):
    center = values - jnp.mean(values, axis=-1, keepdims=True)
    spread = jnp.mean(center * center, axis=-1, keepdims=True)
    return center * lax.rsqrt(spread + EPS) * gain + offset


def node_update(feats, scaled_agg, w_first, bias, w_second, w_third, gain, offset):
    joined = jnp.concatenate([feats, scaled_agg.astype(BF16)], axis=1)
    hidden = jnp.maximum(jnp.dot(joined, w_first, preferred_element_type=F32) + bias, 0.0).astype(BF16)
    middle = jnp.maximum(jnp.dot(hidden, w_second, preferred_element_type=F32), 0.0).astype(BF16)
    output = jnp.dot(middle, w_third, preferred_element_type=F32)
    return layer_norm(feats.astype(F32) + output, gain, offset).astype(BF16)


def order_rows(key_row, key_col, other_col, live_row, live_col, lanes, low, start):
    slots = key_col.shape[0]
    iota = lambda shape, axis: lax.broadcasted_iota(jnp.int32, shape, axis)
    lane = iota((slots, lanes), 1)
    before = (key_row == key_col) & (iota((slots, slots), 1) < iota((slots, slots), 0))
    within = jnp.sum(jnp.where(before, live_row, 0), axis=1, keepdims=True)
    counts = jnp.sum(jnp.where(lane == key_col, live_col, 0), axis=0, keepdims=True)
    counts_col = jnp.sum(jnp.where(iota((lanes, slots), 0) == key_row, live_row, 0), axis=1, keepdims=True)
    steps, steps_col = (counts + 1) >> 1, (counts_col + 1) >> 1
    floor = jnp.where(key_col >= low, low, 0)
    chosen = (lane < key_col) & (lane >= floor)
    base_col = jnp.sum(jnp.where(chosen, steps, 0), axis=1, keepdims=True) + jnp.where(key_col >= low, start, 0)
    place = jnp.where(live_col > 0, base_col * 2 + within, -1)
    hit = place == lane
    index = jnp.sum(jnp.where(hit, iota((slots, lanes), 0) - slots, 0), axis=0, keepdims=True) + slots
    other = jnp.sum(jnp.where(hit, other_col, 0), axis=0, keepdims=True)
    opens = (place == lane * 2) & (within == 0)
    carry = 1 - jnp.sum(jnp.where(opens, 1, 0), axis=0, keepdims=True)
    above, below = iota((lanes, lanes), 0), iota((lanes, lanes), 1)
    upto = (above <= below) & ((above >= low) == (below >= low))
    ends = jnp.sum(jnp.where(upto, steps_col, 0), axis=0, keepdims=True)
    ends += jnp.where(iota((1, lanes), 1) >= low, start, 0)
    last = jnp.maximum(ends - 1, 0)
    filled = jnp.where(counts > 0, 1, 0)
    return [index, other, carry, last, filled]


def kernel(
    dims,
    cb_s, rb_s, cb_v, rb_v, count_s,
    vf_hbm, cf, coef_hbm,
    cw1, cbias, cw2, cw3, cgain, cshift,
    con_out, agg_out,
    raw, half, scan, paired, feat, result, part, arrive, window, conbuf,
    order_v, order_s,
    raw_sem, feat_sem, order_sem, out_sem, psend, precv, wsend, wrecv,
):
    nb, nc, slots, size, cols, fpairs, pairs, lanes, chunks = dims
    band = lax.axis_index("band")
    cut = lax.axis_index("cuts")
    has_next = band < nb - 1
    has_prev = band > 0

    feat_copy = pltpu.make_async_copy(vf_hbm, feat, feat_sem)
    feat_copy.start()

    def raw_copy(i):
        piece = pl.ds(i * CHUNK, CHUNK)
        return pltpu.make_async_copy(coef_hbm.at[piece], raw.at[piece], raw_sem.at[i])

    for i in range(chunks):
        raw_copy(i).start()

    barrier = pltpu.get_barrier_semaphore()
    for d in range(1, nc):
        pl.semaphore_signal(barrier, inc=1, device_id=(band, lax.rem(cut + d, nc)), device_id_type=MESH)

    @pl.when(has_next)
    def _():
        for d in range(nc):
            pl.semaphore_signal(barrier, inc=1, device_id=(band + 1, lax.rem(cut + d, nc)), device_id_type=MESH)

    @pl.when(has_prev)
    def _():
        for d in range(nc):
            pl.semaphore_signal(barrier, inc=1, device_id=(band - 1, lax.rem(cut + d, nc)), device_id_type=MESH)

    row_c = cb_v[...]
    row_r = rb_v[...]
    diagonal = lax.broadcasted_iota(jnp.int32, (slots, slots), 0) == lax.broadcasted_iota(jnp.int32, (slots, slots), 1)
    col_c = jnp.sum(jnp.where(diagonal, row_c, 0), axis=1, keepdims=True)
    col_r = jnp.sum(jnp.where(diagonal, row_r, 0), axis=1, keepdims=True)
    count = count_s[0]
    early = chunks // 2 * CHUNK
    live_row = jnp.where(lax.broadcasted_iota(jnp.int32, (1, slots), 1) < count, 1, 0)
    live_col = jnp.where(lax.broadcasted_iota(jnp.int32, (slots, 1), 0) < count, 1, 0)
    keys = 2 * nc * (part.shape[1] // size)
    late_row = jnp.where(lax.broadcasted_iota(jnp.int32, (1, slots), 1) >= early, keys, 0)
    late_col = jnp.where(lax.broadcasted_iota(jnp.int32, (slots, 1), 0) >= early, keys, 0)
    rows = order_rows(row_r + late_row, col_r + late_col, col_c, live_row, live_col, lanes, keys, fpairs // 2)
    rows += order_rows(row_c, col_c, col_r, live_row, live_col, lanes, lanes, 0)
    rows += [jnp.zeros((1, lanes), jnp.int32)] * (16 - len(rows))
    order_v[...] = jnp.concatenate(rows, axis=0)
    order_copy = pltpu.make_async_copy(order_v, order_s, order_sem)
    order_copy.start()

    half[slots] = jnp.zeros((size, size), BF16)

    @pl.when(jnp.logical_not(has_prev))
    def _():
        arrive[pl.ds(nc, nc)] = jnp.zeros((nc,) + arrive.shape[1:], BF16)

    @pl.when(jnp.logical_not(has_next))
    def _():
        window[pl.ds(nc, nc)] = jnp.zeros((nc,) + window.shape[1:], BF16)

    def convert(i, _):
        raw_copy(i).wait()

        def some(j, _):
            for u in range(UNROLL):
                at = i * CHUNK + j * UNROLL + u
                half[at] = raw[at].astype(F32).astype(BF16)
            return 0

        lax.fori_loop(0, CHUNK // UNROLL, some, 0)
        return 0

    lax.fori_loop(0, chunks // 2, convert, 0)
    feat_copy.wait()
    order_copy.wait()

    def forward(k, carry):
        for u in range(FORWARD):
            at = k * FORWARD + u
            left = jnp.concatenate([half[order_s[0, 2 * at]], half[order_s[0, 2 * at + 1]]], axis=1)
            right = jnp.concatenate([feat[order_s[1, 2 * at]], feat[order_s[1, 2 * at + 1]]], axis=0)
            term = jnp.dot(left, right, preferred_element_type=F32)
            carry = carry * order_s[2, at].astype(F32) + term
            scan[at] = carry
        return carry

    turns = fpairs // FORWARD
    carry = lax.fori_loop(0, turns // 2, forward, jnp.zeros(scan.shape[1:], F32))
    lax.fori_loop(chunks // 2, chunks, convert, 0)
    lax.fori_loop(turns // 2, turns, forward, carry)

    blocks = part.shape[1] // size

    def fill(q):
        for e in range(blocks):
            r = q * blocks + e
            sums = scan[order_s[3, r]] * order_s[4, r].astype(F32)
            sums += scan[order_s[3, keys + r]] * order_s[4, keys + r].astype(F32)
            part[q, e * size : (e + 1) * size] = sums.astype(BF16)

    def part_send(d, ahead):
        to = lax.rem(cut + d, nc)
        q = ahead * nc + d
        return pltpu.make_async_remote_copy(
            src_ref=part.at[ahead * nc + to], dst_ref=arrive.at[ahead * nc + cut],
            send_sem=psend.at[q], recv_sem=precv.at[ahead * nc + cut],
            device_id=(band + ahead, to), device_id_type=MESH)

    def part_wait(src, ahead):
        pltpu.make_async_remote_copy(
            src_ref=part.at[0], dst_ref=arrive.at[ahead * nc + src],
            send_sem=psend.at[0], recv_sem=precv.at[ahead * nc + src],
            device_id=(band, cut), device_id_type=MESH).wait_recv()

    for q in range(2 * nc):
        fill(q)

    expected = (nc - 1) + jnp.where(has_next, nc, 0) + jnp.where(has_prev, nc, 0)
    pl.semaphore_wait(barrier, expected)

    @pl.when(has_next)
    def _():
        for d in range(nc):
            part_send(d, 1).start()

    for d in range(1, nc):
        part_send(d, 0).start()

    def pair_up(p, _):
        for u in range(2):
            k = p * 2 + u
            left = half[order_s[5, 2 * k]].T
            right = half[order_s[5, 2 * k + 1]].T
            paired[k, :, :size] = left
            paired[k, :, size:] = right
        return 0

    lax.fori_loop(0, pairs // 4, pair_up, 0)

    total = part[cut].astype(F32)
    for d in range(1, nc):
        src = lax.rem(cut + d, nc)
        part_wait(src, 0)
        total += arrive[src].astype(F32)

    @pl.when(has_prev)
    def _():
        for src in range(nc):
            part_wait(src, 1)

    for src in range(nc):
        total += arrive[nc + src].astype(F32)

    con_new = node_update(
        cf[...], total * (1.0 / math.sqrt(size * slots)), cw1[...], cbias[...], cw2[...], cw3[...], cgain[...], cshift[...])
    conbuf[...] = con_new
    con_out[...] = con_new
    window[cut] = con_new

    def win_send(d, back):
        to = lax.rem(cut + d, nc)
        return pltpu.make_async_remote_copy(
            src_ref=conbuf, dst_ref=window.at[back * nc + cut],
            send_sem=wsend.at[back * nc + d], recv_sem=wrecv.at[back * nc + cut],
            device_id=(band - back, to), device_id_type=MESH)

    def win_wait(src, back):
        pltpu.make_async_remote_copy(
            src_ref=conbuf, dst_ref=window.at[back * nc + src],
            send_sem=wsend.at[0], recv_sem=wrecv.at[back * nc + src],
            device_id=(band, cut), device_id_type=MESH).wait_recv()

    @pl.when(has_prev)
    def _():
        for d in range(nc):
            win_send(d, 1).start()

    for d in range(1, nc):
        win_send(d, 0).start()

    lax.fori_loop(pairs // 4, pairs // 2, pair_up, 0)

    @pl.when(has_next)
    def _():
        for d in range(nc):
            part_send(d, 1).wait_send()

    for d in range(1, nc):
        part_send(d, 0).wait_send()
        win_wait(lax.rem(cut + d, nc), 0)

    @pl.when(has_next)
    def _():
        for src in range(nc):
            win_wait(src, 1)

    def row_block(r):
        if blocks == 1:
            return window[r]
        return window[r // blocks, pl.ds(pl.multiple_of(r % blocks * size, size), size)]

    def back(k, carry):
        for u in range(BACK):
            at = k * BACK + u
            right = jnp.concatenate([row_block(order_s[6, 2 * at]), row_block(order_s[6, 2 * at + 1])], axis=0)
            term = jnp.dot(paired[at], right, preferred_element_type=F32)
            carry = carry * order_s[7, at].astype(F32) + term
            scan[at] = carry
        return carry

    lax.fori_loop(0, pairs // BACK, back, jnp.zeros(scan.shape[1:], F32))

    scale = 1.0 / math.sqrt(4 * size)
    def out_copy(i):
        piece = pl.ds(i * GATHER, GATHER)
        return pltpu.make_async_copy(result.at[piece], agg_out.at[piece], out_sem.at[i])

    def gather(i, _):
        for u in range(GATHER):
            c = i * GATHER + u
            result[c] = (scan[order_s[8, c]] * (order_s[9, c].astype(F32) * scale)).astype(BF16)
        out_copy(i).start()
        return 0

    lax.fori_loop(0, cols // GATHER, gather, 0)

    @pl.when(has_prev)
    def _():
        for d in range(nc):
            win_send(d, 1).wait_send()

    for d in range(1, nc):
        win_send(d, 0).wait_send()

    def finish(i, _):
        out_copy(i).wait()
        return 0

    lax.fori_loop(0, cols // GATHER, finish, 0)


def column_kernel(feat, agg, con, vw1, vbias, vw2, vw3, vgain, vshift, con_out, var_out):
    @pl.when(pl.program_id(0) == 0)
    def _():
        con_out[...] = con[...]

    var_out[...] = node_update(
        feat[...], agg[...], vw1[...], vbias[...], vw2[...], vw3[...], vgain[...], vshift[...])


def on_device(
    nb, nc,
    var_feat, con_feat, slot_column_block, slot_constraint_block, block_count, incidence_coefficients,
    con_first, con_bias, con_second, con_third, con_gain, con_shift,
    var_first, var_bias, var_second, var_third, var_gain, var_shift,
):
    width = var_feat.shape[1]
    slots = slot_column_block.shape[0]
    size = incidence_coefficients.shape[1]
    cols = var_feat.shape[0] // size
    rows = con_feat.shape[0]
    rblocks = 2 * nc * (rows // size)
    early = slots // CHUNK // 2 * CHUNK
    fpairs = -(-(slots - early + rblocks) // (2 * FORWARD)) * FORWARD * 2
    pairs = -(-(slots + cols) // (2 * BACK)) * BACK
    lanes = -(-max(2 * pairs, 2 * fpairs, 2 * rblocks) // 128) * 128
    chunks = slots // CHUNK
    dims = (nb, nc, slots, size, cols, fpairs, pairs, lanes, chunks)
    smem = pl.BlockSpec(memory_space=pltpu.SMEM)
    vmem = pl.BlockSpec(memory_space=pltpu.VMEM)
    hbm = pl.BlockSpec(memory_space=pl.ANY)
    row = lambda v: v.reshape(1, -1)
    con_new, agg = pl.pallas_call(
        functools.partial(kernel, dims),
        out_shape=(
            jax.ShapeDtypeStruct(con_feat.shape, BF16),
            jax.ShapeDtypeStruct((cols, size, width), BF16),
        ),
        in_specs=[smem, smem, vmem, vmem, smem, hbm, vmem, hbm] + [vmem] * 6,
        out_specs=(vmem, hbm),
        scratch_shapes=[
            pltpu.VMEM((slots, size, size), jnp.int32),
            pltpu.VMEM((slots + 1, size, size), BF16),
            pltpu.VMEM((max(fpairs, pairs), size, width), F32),
            pltpu.VMEM((pairs, size, 2 * size), BF16),
            pltpu.VMEM((cols, size, width), BF16),
            pltpu.VMEM((cols, size, width), BF16),
            pltpu.VMEM((2 * nc, rows, width), BF16),
            pltpu.VMEM((2 * nc, rows, width), BF16),
            pltpu.VMEM((2 * nc, rows, width), BF16),
            pltpu.VMEM((rows, width), BF16),
            pltpu.VMEM((16, lanes), jnp.int32),
            pltpu.SMEM((16, lanes), jnp.int32),
            pltpu.SemaphoreType.DMA((chunks,)),
            pltpu.SemaphoreType.DMA,
            pltpu.SemaphoreType.DMA,
            pltpu.SemaphoreType.DMA((cols // GATHER,)),
            pltpu.SemaphoreType.DMA((2 * nc,)),
            pltpu.SemaphoreType.DMA((2 * nc,)),
            pltpu.SemaphoreType.DMA((2 * nc,)),
            pltpu.SemaphoreType.DMA((2 * nc,)),
        ],
        compiler_params=pltpu.CompilerParams(
            collective_id=0, has_side_effects=True, vmem_limit_bytes=63 * 1024 * 1024),
        name="layer",
    )(
        slot_column_block, slot_constraint_block, row(slot_column_block), row(slot_constraint_block), block_count,
        var_feat.reshape(cols, size, width), con_feat, incidence_coefficients,
        con_first, row(con_bias), con_second, con_third, row(con_gain), row(con_shift),
    )
    weights = (var_first, row(var_bias), var_second, var_third, row(var_gain), row(var_shift))
    moving = pl.BlockSpec((STEP * size, width), lambda i: (i, 0))
    still = lambda v: pl.BlockSpec(v.shape, lambda i: (0, 0))
    return pl.pallas_call(
        column_kernel,
        grid=(cols // STEP,),
        out_shape=(
            jax.ShapeDtypeStruct(con_feat.shape, BF16),
            jax.ShapeDtypeStruct(var_feat.shape, BF16),
        ),
        in_specs=[moving, moving, still(con_new)] + [still(w) for w in weights],
        out_specs=(still(con_new), moving),
        compiler_params=pltpu.CompilerParams(vmem_limit_bytes=63 * 1024 * 1024),
        name="columns",
    )(var_feat, agg.reshape(var_feat.shape), con_new, *weights)


def solution(mesh):
    both = P(("band", "cuts"))
    wide = P(("band", "cuts"), None)
    in_specs = (wide, wide, both, both, both, P(("band", "cuts"), None, None)) + (P(),) * 12
    body = functools.partial(on_device, mesh.shape["band"], mesh.shape["cuts"])
    return jax.shard_map(body, mesh=mesh, in_specs=in_specs, out_specs=(wide, wide), check_vma=False)
```

profile of v0, /device:TPU:0, one launch (start us, length us, event | category | flops | bytes accessed | tf_op | source)
XLA Modules:
  0.0 31.3 jit_solution(3653318673264582946)
XLA Ops:
  1.3 23.9 %layer.1 = (bf16[128,128]{1,0:T(8,128)(2,1)}, bf16[40,128,128]{2,1,0:T(8,128)(2,1)}) custom-call(s32[160]{0:T(256)} %cb_s.1, s32[160]{0:T(256)} %rb_s.1, s32[1,160]{1,0:T(1,128)} %bitcast.12, s32[1,160]{1,0:T(1,128)} %bitcast.13, s32[1]{0:T(128)S(6)} %copy.20.count_s, bf16[40,128,128]{2,1,0:T(8,128)(2,1)} %bitcast.10, bf16[128,128]{1,0:T(8,128)(2,1)} %cf.1, ...), custom_call_target="tpu_custom_call" | custom-call | tf_op jit(solution)/shard_map/layer/pallas_call | solution.py:345
  25.2 6.1 %columns.1 = (bf16[128,128]{1,0:T(8,128)(2,1)}, bf16[5120,128]{1,0:T(8,128)(2,1)}) custom-call(bf16[5120,128]{1,0:T(8,128)(2,1)} %feat.1, bf16[5120,128]{1,0:T(8,128)(2,1)} %bitcast.11, bf16[128,128]{1,0:T(8,128)(2,1)} %get-tuple-element.5.con, bf16[256,256]{1,0:T(8,128)(2,1)} %vw1.1, f32[1,256]{1,0:T(1,128)} %bitcast.14, bf16[256,256]{1,0:T(8,128)(2,1)} %vw2.1, ...), custom_call_target="tpu_custom_call" | custom-call | tf_op jit(solution)/shard_map/columns/pallas_call | solution.py:386
where the time goes:
time: 31.5 us; the launch traced here: 31.3 us
  Pallas kernels  30 us (95%)
  between operations  1.29 us (4%)
    pallas_call x1, Pallas kernels, on_device(): pl.pallas_call(functools.partial(kernel, dims), out_shape=(jax.ShapeDtype...  23.9 us
    pallas_call x1, Pallas kernels, on_device(): pl.pallas_call(column_kernel, grid=(cols // STEP,), out_shape=(jax.ShapeD...  6.11 us

commit v1 on v0

v1 whole, which is shorter than its diff:
```python
import functools
import math

import jax
import jax.numpy as jnp
from jax import lax
from jax.experimental import pallas as pl
from jax.experimental.pallas import tpu as pltpu
from jax.sharding import PartitionSpec as P

EPS = 1e-05
F32 = jnp.float32
BF16 = jnp.bfloat16
FP8 = jnp.float8_e4m3fn
MESH = pl.DeviceIdType.MESH
CHUNK = 16
UNROLL = 8
FORWARD = 22
BACK = 25
PAIR = 5
GATHER = 8
TILE = 512
FEAT_SCALE = 64.0
CON_SCALE = 16.0
LOW_SCALE = 16.0


def layer_norm(values, gain, offset):
    center = values - jnp.mean(values, axis=-1, keepdims=True)
    spread = jnp.mean(center * center, axis=-1, keepdims=True)
    return center * lax.rsqrt(spread + EPS) * gain + offset


def node_update(feats, scaled_agg, w_first, bias, w_second, w_third, gain, offset):
    joined = jnp.concatenate([feats, scaled_agg.astype(BF16)], axis=1)
    hidden = jnp.maximum(jnp.dot(joined, w_first, preferred_element_type=F32) + bias, 0.0).astype(BF16)
    middle = jnp.maximum(jnp.dot(hidden, w_second, preferred_element_type=F32), 0.0).astype(BF16)
    output = jnp.dot(middle, w_third, preferred_element_type=F32)
    return layer_norm(feats.astype(F32) + output, gain, offset).astype(BF16)


def split(values, scale):
    scaled = values.astype(F32) * scale
    high = scaled.astype(FP8)
    low = ((scaled - high.astype(F32)) * LOW_SCALE).astype(FP8)
    return high, low


def join(products, width):
    return products[:, :width] + products[:, width:] * (1.0 / LOW_SCALE)


def order_rows(key_row, key_col, other_col, live_row, live_col, lanes, low, start):
    slots = key_col.shape[0]
    iota = lambda shape, axis: lax.broadcasted_iota(jnp.int32, shape, axis)
    lane = iota((slots, lanes), 1)
    before = (key_row == key_col) & (iota((slots, slots), 1) < iota((slots, slots), 0))
    within = jnp.sum(jnp.where(before, live_row, 0), axis=1, keepdims=True)
    counts = jnp.sum(jnp.where(lane == key_col, live_col, 0), axis=0, keepdims=True)
    counts_col = jnp.sum(jnp.where(iota((lanes, slots), 0) == key_row, live_row, 0), axis=1, keepdims=True)
    steps, steps_col = (counts + 1) >> 1, (counts_col + 1) >> 1
    floor = jnp.where(key_col >= low, low, 0)
    chosen = (lane < key_col) & (lane >= floor)
    base_col = jnp.sum(jnp.where(chosen, steps, 0), axis=1, keepdims=True) + jnp.where(key_col >= low, start, 0)
    place = jnp.where(live_col > 0, base_col * 2 + within, -1)
    hit = place == lane
    index = jnp.sum(jnp.where(hit, iota((slots, lanes), 0) - slots, 0), axis=0, keepdims=True) + slots
    other = jnp.sum(jnp.where(hit, other_col, 0), axis=0, keepdims=True)
    opens = (place == lane * 2) & (within == 0)
    carry = 1 - jnp.sum(jnp.where(opens, 1, 0), axis=0, keepdims=True)
    above, below = iota((lanes, lanes), 0), iota((lanes, lanes), 1)
    upto = (above <= below) & ((above >= low) == (below >= low))
    ends = jnp.sum(jnp.where(upto, steps_col, 0), axis=0, keepdims=True)
    ends += jnp.where(iota((1, lanes), 1) >= low, start, 0)
    last = jnp.maximum(ends - 1, 0)
    filled = jnp.where(counts > 0, 1, 0)
    rows = [index, other, carry, last, filled]
    return jnp.concatenate(rows + [jnp.zeros((1, lanes), jnp.int32)] * (8 - len(rows)), axis=0)


def kernel(
    dims,
    cb_hbm, rb_hbm, count_s, vf_hbm, cf_hbm, coef_hbm, *refs,
):
    nb, nc, slots, size, cols, fpairs, pairs, lanes, chunks = dims
    con_weights_hbm, var_weights_hbm, refs = refs[:6], refs[6:12], refs[12:]
    con_out, agg_out, feat, refs = refs[0], refs[1], refs[2], refs[3:]
    var_weights, refs = refs[:6], refs[6:]
    cb_v, rb_v, cf, con_weights, refs = refs[0], refs[1], refs[2], refs[3:9], refs[9:]
    (
        raw, half, scan, paired, feat8, part, arrive, window, win8, conbuf,
        orderf_v, orderf_s, orderb_v, orderb_s,
        raw_sem, feat_sem, small_sem, weight_sem, order_sem, psend, precv, wsend, wrecv,
    ) = refs
    band = lax.axis_index("band")
    cut = lax.axis_index("cuts")
    has_next = band < nb - 1
    has_prev = band > 0
    width = feat.shape[1]

    small = [
        pltpu.make_async_copy(src, dst, small_sem.at[i])
        for i, (src, dst) in enumerate(((cb_hbm, cb_v), (rb_hbm, rb_v)))
    ]
    for copy in small:
        copy.start()

    def raw_copy(i):
        piece = pl.ds(i * CHUNK, CHUNK)
        return pltpu.make_async_copy(coef_hbm.at[piece], raw.at[piece], raw_sem.at[i])

    for i in range(chunks // 2):
        raw_copy(i).start()
    feat_copy = pltpu.make_async_copy(vf_hbm, feat, feat_sem)
    feat_copy.start()
    for i in range(chunks // 2, chunks):
        raw_copy(i).start()
    weights = [
        pltpu.make_async_copy(src, dst, weight_sem.at[i])
        for i, (src, dst) in enumerate(
            zip((cf_hbm, *con_weights_hbm, *var_weights_hbm), (cf, *con_weights, *var_weights)))
    ]
    for copy in weights:
        copy.start()

    barrier = pltpu.get_barrier_semaphore()
    for d in range(1, nc):
        pl.semaphore_signal(barrier, inc=1, device_id=(band, lax.rem(cut + d, nc)), device_id_type=MESH)

    @pl.when(has_next)
    def _():
        for d in range(nc):
            pl.semaphore_signal(barrier, inc=1, device_id=(band + 1, lax.rem(cut + d, nc)), device_id_type=MESH)

    @pl.when(has_prev)
    def _():
        for d in range(nc):
            pl.semaphore_signal(barrier, inc=1, device_id=(band - 1, lax.rem(cut + d, nc)), device_id_type=MESH)

    half[slots] = jnp.zeros((size, size), FP8)

    @pl.when(jnp.logical_not(has_prev))
    def _():
        arrive[pl.ds(nc, nc)] = jnp.zeros((nc,) + arrive.shape[1:], BF16)

    @pl.when(jnp.logical_not(has_next))
    def _():
        window[pl.ds(nc, nc)] = jnp.zeros((nc,) + window.shape[1:], BF16)

    for copy in small:
        copy.wait()
    row_c = cb_v[...]
    row_r = rb_v[...]
    diagonal = lax.broadcasted_iota(jnp.int32, (slots, slots), 0) == lax.broadcasted_iota(jnp.int32, (slots, slots), 1)
    col_c = jnp.sum(jnp.where(diagonal, row_c, 0), axis=1, keepdims=True)
    col_r = jnp.sum(jnp.where(diagonal, row_r, 0), axis=1, keepdims=True)
    count = count_s[0]
    early = chunks // 2 * CHUNK
    live_row = jnp.where(lax.broadcasted_iota(jnp.int32, (1, slots), 1) < count, 1, 0)
    live_col = jnp.where(lax.broadcasted_iota(jnp.int32, (slots, 1), 0) < count, 1, 0)
    blocks = part.shape[1] // size
    keys = 2 * nc * blocks
    late_row = jnp.where(lax.broadcasted_iota(jnp.int32, (1, slots), 1) >= early, keys, 0)
    late_col = jnp.where(lax.broadcasted_iota(jnp.int32, (slots, 1), 0) >= early, keys, 0)
    orderf_v[...] = order_rows(row_r + late_row, col_r + late_col, col_c, live_row, live_col, lanes, keys, fpairs // 2)
    orderf_copy = pltpu.make_async_copy(orderf_v, orderf_s, order_sem.at[0])
    orderf_copy.start()

    def convert(i, _):
        raw_copy(i).wait()

        def some(j, _):
            for u in range(UNROLL):
                at = i * CHUNK + j * UNROLL + u
                half[at] = raw[at].astype(F32).astype(FP8)
            return 0

        lax.fori_loop(0, CHUNK // UNROLL, some, 0)
        return 0

    lax.fori_loop(0, chunks // 2, convert, 0)
    feat_copy.wait()

    def split_feat(i, _):
        for u in range(GATHER // 2):
            at = i * (GATHER // 2) + u
            high, low = split(feat[pl.ds(pl.multiple_of(at * size, size), size)], FEAT_SCALE)
            feat8[at, :, :width] = high
            feat8[at, :, width:] = low
        return 0

    lax.fori_loop(0, cols // (GATHER // 2), split_feat, 0)
    orderf_copy.wait()

    def forward(k, carry):
        for u in range(FORWARD):
            at = k * FORWARD + u
            left = jnp.concatenate([half[orderf_s[0, 2 * at]], half[orderf_s[0, 2 * at + 1]]], axis=1)
            right = jnp.concatenate([feat8[orderf_s[1, 2 * at]], feat8[orderf_s[1, 2 * at + 1]]], axis=0)
            term = join(jnp.dot(left, right, preferred_element_type=F32), width)
            carry = carry * orderf_s[2, at].astype(F32) + term
            scan[at] = carry
        return carry

    turns = fpairs // FORWARD
    carry = lax.fori_loop(0, turns // 2, forward, jnp.zeros(scan.shape[1:], F32))
    lax.fori_loop(chunks // 2, chunks, convert, 0)
    lax.fori_loop(turns // 2, turns, forward, carry)

    def fill(q):
        for e in range(blocks):
            r = q * blocks + e
            sums = scan[orderf_s[3, r]] * orderf_s[4, r].astype(F32)
            sums += scan[orderf_s[3, keys + r]] * orderf_s[4, keys + r].astype(F32)
            part[q, e * size : (e + 1) * size] = (sums * (1.0 / FEAT_SCALE)).astype(BF16)

    def part_send(d, ahead):
        to = lax.rem(cut + d, nc)
        q = ahead * nc + d
        return pltpu.make_async_remote_copy(
            src_ref=part.at[ahead * nc + to], dst_ref=arrive.at[ahead * nc + cut],
            send_sem=psend.at[q], recv_sem=precv.at[ahead * nc + cut],
            device_id=(band + ahead, to), device_id_type=MESH)

    def part_wait(src, ahead):
        pltpu.make_async_remote_copy(
            src_ref=part.at[0], dst_ref=arrive.at[ahead * nc + src],
            send_sem=psend.at[0], recv_sem=precv.at[ahead * nc + src],
            device_id=(band, cut), device_id_type=MESH).wait_recv()

    for q in range(2 * nc):
        fill(q)

    expected = (nc - 1) + jnp.where(has_next, nc, 0) + jnp.where(has_prev, nc, 0)
    pl.semaphore_wait(barrier, expected)

    @pl.when(has_next)
    def _():
        for d in range(nc):
            part_send(d, 1).start()

    for d in range(1, nc):
        part_send(d, 0).start()

    orderb_v[...] = order_rows(row_c, col_c, col_r, live_row, live_col, lanes, lanes, 0)
    orderb_copy = pltpu.make_async_copy(orderb_v, orderb_s, order_sem.at[1])
    orderb_copy.start()
    for copy in weights:
        copy.wait()
    orderb_copy.wait()

    def pair_up(p, _):
        for u in range(PAIR):
            k = p * PAIR + u
            paired[k, :, :size] = half[orderb_s[0, 2 * k]].T
            paired[k, :, size:] = half[orderb_s[0, 2 * k + 1]].T
        return 0

    lax.fori_loop(0, pairs // PAIR, pair_up, 0)

    total = part[cut].astype(F32)
    for d in range(1, nc):
        src = lax.rem(cut + d, nc)
        part_wait(src, 0)
        total += arrive[src].astype(F32)

    @pl.when(has_prev)
    def _():
        for src in range(nc):
            part_wait(src, 1)

    for src in range(nc):
        total += arrive[nc + src].astype(F32)

    con_new = node_update(cf[...], total * (1.0 / math.sqrt(size * slots)), *(w[...] for w in con_weights))
    conbuf[...] = con_new
    window[cut] = con_new

    def win_send(d, back):
        to = lax.rem(cut + d, nc)
        return pltpu.make_async_remote_copy(
            src_ref=conbuf, dst_ref=window.at[back * nc + cut],
            send_sem=wsend.at[back * nc + d], recv_sem=wrecv.at[back * nc + cut],
            device_id=(band - back, to), device_id_type=MESH)

    def win_wait(src, back):
        pltpu.make_async_remote_copy(
            src_ref=conbuf, dst_ref=window.at[back * nc + src],
            send_sem=wsend.at[0], recv_sem=wrecv.at[back * nc + src],
            device_id=(band, cut), device_id_type=MESH).wait_recv()

    @pl.when(has_prev)
    def _():
        for d in range(nc):
            win_send(d, 1).start()

    for d in range(1, nc):
        win_send(d, 0).start()

    con_out[...] = con_new

    @pl.when(has_next)
    def _():
        for d in range(nc):
            part_send(d, 1).wait_send()

    for d in range(1, nc):
        part_send(d, 0).wait_send()

    def split_con(q):
        for e in range(blocks):
            high, low = split(window[q, e * size : (e + 1) * size], CON_SCALE)
            win8[q * blocks + e, :, :width] = high
            win8[q * blocks + e, :, width:] = low

    for d in range(1, nc):
        win_wait(lax.rem(cut + d, nc), 0)
    for q in range(nc):
        split_con(q)

    @pl.when(has_next)
    def _():
        for src in range(nc):
            win_wait(src, 1)

    for q in range(nc, 2 * nc):
        split_con(q)

    def back(k, carry):
        for u in range(BACK):
            at = k * BACK + u
            right = jnp.concatenate([win8[orderb_s[1, 2 * at]], win8[orderb_s[1, 2 * at + 1]]], axis=0)
            term = join(jnp.dot(paired[at], right, preferred_element_type=F32), width)
            carry = carry * orderb_s[2, at].astype(F32) + term
            scan[at] = carry
        return carry

    lax.fori_loop(0, pairs // BACK, back, jnp.zeros(scan.shape[1:], F32))

    scale = 1.0 / (CON_SCALE * math.sqrt(4 * size))

    def gather(i, _):
        for u in range(GATHER):
            c = i * GATHER + u
            sums = scan[orderb_s[3, c]] * (orderb_s[4, c].astype(F32) * scale)
            agg_out[pl.ds(pl.multiple_of(c * size, size), size)] = sums.astype(BF16)
        return 0

    lax.fori_loop(0, cols // GATHER, gather, 0)

    @pl.when(has_prev)
    def _():
        for d in range(nc):
            win_send(d, 1).wait_send()

    for d in range(1, nc):
        win_send(d, 0).wait_send()


def column_kernel(
    feat, agg, con, vw1, vbias, vw2, vw3, vgain, vshift, con_out, var_out,
    result, hidden, middle, output, out_sem, con_sem,
):
    con_copy = pltpu.make_async_copy(con, con_out, con_sem)
    con_copy.start()
    tiles = feat.shape[0] // TILE
    piece = lambda i: pl.ds(i * TILE, TILE)

    def out_copy(i):
        return pltpu.make_async_copy(result.at[piece(i)], var_out.at[piece(i)], out_sem.at[i])

    def first(i):
        joined = jnp.concatenate([feat[piece(i)], agg[piece(i)]], axis=1)
        sums = jnp.dot(joined, vw1[...], preferred_element_type=F32) + vbias[...]
        hidden[i % 2] = jnp.maximum(sums, 0.0).astype(BF16)

    def second(i):
        sums = jnp.dot(hidden[i % 2], vw2[...], preferred_element_type=F32)
        middle[i % 2] = jnp.maximum(sums, 0.0).astype(BF16)

    def third(i):
        sums = jnp.dot(middle[i % 2], vw3[...], preferred_element_type=F32)
        output[i % 2] = feat[piece(i)].astype(F32) + sums

    def norm(i):
        result[piece(i)] = layer_norm(output[i % 2], vgain[...], vshift[...]).astype(BF16)
        out_copy(i).start()

    stages = (norm, 3), (third, 2), (second, 1), (first, 0)
    for t in range(tiles + len(stages) - 1):
        for stage, delay in stages:
            if 0 <= t - delay < tiles:
                stage(t - delay)

    con_copy.wait()
    for i in range(tiles):
        out_copy(i).wait()


def on_device(
    nb, nc,
    var_feat, con_feat, slot_column_block, slot_constraint_block, block_count, incidence_coefficients,
    con_first, con_bias, con_second, con_third, con_gain, con_shift,
    var_first, var_bias, var_second, var_third, var_gain, var_shift,
):
    width = var_feat.shape[1]
    slots = slot_column_block.shape[0]
    size = incidence_coefficients.shape[1]
    cols = var_feat.shape[0] // size
    rows = con_feat.shape[0]
    rblocks = 2 * nc * (rows // size)
    early = slots // CHUNK // 2 * CHUNK
    fpairs = -(-(slots - early + rblocks) // (2 * FORWARD)) * FORWARD * 2
    pairs = -(-(slots + cols) // (2 * BACK)) * BACK
    lanes = -(-max(2 * pairs, 2 * fpairs, 2 * rblocks) // 128) * 128
    chunks = slots // CHUNK
    dims = (nb, nc, slots, size, cols, fpairs, pairs, lanes, chunks)
    vmem = pl.BlockSpec(memory_space=pltpu.VMEM)
    hbm = pl.BlockSpec(memory_space=pl.ANY)
    row = lambda v: v.reshape(1, -1)
    con_weights = (con_first, row(con_bias), con_second, con_third, row(con_gain), row(con_shift))
    var_weights = (var_first, row(var_bias), var_second, var_third, row(var_gain), row(var_shift))
    held = lambda v: pltpu.with_memory_space_constraint(v, pltpu.HBM)
    like = lambda v: pltpu.VMEM(v.shape, v.dtype)
    handed = pl.pallas_call(
        functools.partial(kernel, dims),
        out_shape=(
            pltpu.VMEM(con_feat.shape, BF16),
            pltpu.VMEM(var_feat.shape, BF16),
            like(var_feat),
            *(like(w) for w in var_weights),
        ),
        in_specs=[hbm] * 2 + [pl.BlockSpec(memory_space=pltpu.SMEM)] + [hbm] * 15,
        out_specs=(vmem,) * 9,
        scratch_shapes=[
            pltpu.VMEM((1, slots), jnp.int32),
            pltpu.VMEM((1, slots), jnp.int32),
            like(con_feat),
            *(like(w) for w in con_weights),
            pltpu.VMEM((slots, size, size), jnp.int32),
            pltpu.VMEM((slots + 1, size, size), FP8),
            pltpu.VMEM((max(fpairs, pairs), size, width), F32),
            pltpu.VMEM((pairs, size, 2 * size), FP8),
            pltpu.VMEM((cols, size, 2 * width), FP8),
            pltpu.VMEM((2 * nc, rows, width), BF16),
            pltpu.VMEM((2 * nc, rows, width), BF16),
            pltpu.VMEM((2 * nc, rows, width), BF16),
            pltpu.VMEM((rblocks, size, 2 * width), FP8),
            pltpu.VMEM((rows, width), BF16),
            pltpu.VMEM((8, lanes), jnp.int32),
            pltpu.SMEM((8, lanes), jnp.int32),
            pltpu.VMEM((8, lanes), jnp.int32),
            pltpu.SMEM((8, lanes), jnp.int32),
            pltpu.SemaphoreType.DMA((chunks,)),
            pltpu.SemaphoreType.DMA,
            pltpu.SemaphoreType.DMA((2,)),
            pltpu.SemaphoreType.DMA((13,)),
            pltpu.SemaphoreType.DMA((2,)),
            pltpu.SemaphoreType.DMA((2 * nc,)),
            pltpu.SemaphoreType.DMA((2 * nc,)),
            pltpu.SemaphoreType.DMA((2 * nc,)),
            pltpu.SemaphoreType.DMA((2 * nc,)),
        ],
        compiler_params=pltpu.CompilerParams(
            collective_id=0, has_side_effects=True, vmem_limit_bytes=48 * 1024 * 1024),
        name="layer",
    )(
        *map(held, (row(slot_column_block), row(slot_constraint_block))), block_count,
        *map(held, (var_feat, con_feat, incidence_coefficients, *con_weights, *var_weights)),
    )
    con_new, agg, feat, *weights = (pltpu.with_memory_space_constraint(v, pltpu.VMEM) for v in handed)
    return pl.pallas_call(
        column_kernel,
        out_shape=(
            jax.ShapeDtypeStruct(con_feat.shape, BF16),
            jax.ShapeDtypeStruct(var_feat.shape, BF16),
        ),
        in_specs=[vmem] * 9,
        out_specs=(hbm, hbm),
        scratch_shapes=[
            pltpu.VMEM(var_feat.shape, BF16),
            pltpu.VMEM((2, TILE, var_first.shape[1]), BF16),
            pltpu.VMEM((2, TILE, var_second.shape[1]), BF16),
            pltpu.VMEM((2, TILE, width), F32),
            pltpu.SemaphoreType.DMA((var_feat.shape[0] // TILE,)),
            pltpu.SemaphoreType.DMA,
        ],
        compiler_params=pltpu.CompilerParams(vmem_limit_bytes=32 * 1024 * 1024),
        name="columns",
    )(feat, agg, con_new, *weights)


def solution(mesh):
    both = P(("band", "cuts"))
    wide = P(("band", "cuts"), None)
    in_specs = (wide, wide, both, both, both, P(("band", "cuts"), None, None)) + (P(),) * 12
    body = functools.partial(on_device, mesh.shape["band"], mesh.shape["cuts"])
    return jax.shard_map(body, mesh=mesh, in_specs=in_specs, out_specs=(wide, wide), check_vma=False)
```

time: 31.5 us -> 25.6 us (0.81)
  Pallas kernels: 30 us -> 24.2 us
    pallas_call x2, Pallas kernels: 30 us -> 24.2 us  [the longest x1 20.9 us: on_device(): pl.pallas_call(functools.partial(kernel, dims), out_shape=(pltpu.VMEM(con...]
where the time goes in v1:
time: 25.6 us; the launch traced here: 25.5 us
  Pallas kernels  24.2 us (95%)
  between operations  1.29 us (5%)
    pallas_call x1, Pallas kernels, on_device(): pl.pallas_call(functools.partial(kernel, dims), out_shape=(pltpu.VMEM(con...  20.9 us
    pallas_call x1, Pallas kernels, on_device(): pl.pallas_call(column_kernel, out_shape=(jax.ShapeDtypeStruct(con_feat.sh...  3.27 us

profile of v1, /device:TPU:0, one launch (start us, length us, event | category | flops | bytes accessed | tf_op | source)
XLA Modules:
  0.0 25.5 jit_solution(8526764657553297597)
XLA Ops:
  1.3 20.9 %layer.1 = (bf16[128,128]{1,0:T(8,128)(2,1)S(1)}, bf16[5120,128]{1,0:T(8,128)(2,1)S(1)}, bf16[5120,128]{1,0:T(8,128)(2,1)S(1)}, bf16[256,256]{1,0:T(8,128)(2,1)S...) custom-call(s32[1,160]{1,0:T(1,128)} %bitcast.8, ...), custom_call_target="tpu_custom_call" | custom-call | tf_op jit(solution)/shard_map/layer/pallas_call | solution.py:425
  22.2 3.3 %columns.1 = (bf16[128,128]{1,0:T(8,128)(2,1)}, bf16[5120,128]{1,0:T(8,128)(2,1)}) custom-call(bf16[5120,128]{1,0:T(8,128)(2,1)S(1)} %get-tuple-element.11.feat, bf16[5120,128]{1,0:T(8,128)(2,1)S(1)} %get-tuple-element.12.agg, bf16[128,128]{1,0:T(8,128)(2,1)S(1)} %get-tuple-element.13.con, bf16[256,256]{1,0:T(8,128)(2,1)S(1)} %get-tuple-element.14.vw1, ...), custom_call_target="tpu_custom_call" | custom-call | tf_op jit(solution)/shard_map/columns/pallas_call | solution.py:472

commit v2 on v1

v2 whole, which is shorter than its diff:
```python
import functools
import math

import jax
import jax.numpy as jnp
from jax import lax
from jax.experimental import pallas as pl
from jax.experimental.pallas import tpu as pltpu
from jax.sharding import PartitionSpec as P

EPS = 1e-05
F32 = jnp.float32
BF16 = jnp.bfloat16
MESH = pl.DeviceIdType.MESH
CHUNK = 16
UNROLL = 8
BACK = 50
PAIR = 5
BASE = 4
AHEAD = 4
TILE = 512


def layer_norm(values, gain, offset):
    center = values - jnp.mean(values, axis=-1, keepdims=True)
    spread = jnp.mean(center * center, axis=-1, keepdims=True)
    return center * lax.rsqrt(spread + EPS) * gain + offset


def node_update(feats, scaled_agg, w_first, bias, w_second, w_third, gain, offset):
    joined = jnp.concatenate([feats, scaled_agg.astype(BF16)], axis=1)
    hidden = jnp.maximum(jnp.dot(joined, w_first, preferred_element_type=F32) + bias, 0.0).astype(BF16)
    middle = jnp.maximum(jnp.dot(hidden, w_second, preferred_element_type=F32), 0.0).astype(BF16)
    output = jnp.dot(middle, w_third, preferred_element_type=F32)
    return layer_norm(feats.astype(F32) + output, gain, offset).astype(BF16)


def order_rows(key_row, key_col, other_col, live_row, live_col, lanes, keys, starts, empty):
    slots = key_col.shape[0]
    iota = lambda shape, axis: lax.broadcasted_iota(jnp.int32, shape, axis)

    def by_group(key, values):
        out = values[0]
        for g in range(1, len(values)):
            out = jnp.where(key >= g * keys, values[g], out)
        return out

    floors = tuple(g * keys for g in range(len(starts)))
    lane = iota((slots, lanes), 1)
    before = (key_row == key_col) & (iota((slots, slots), 1) < iota((slots, slots), 0))
    within = jnp.sum(jnp.where(before, live_row, 0), axis=1, keepdims=True)
    counts = jnp.sum(jnp.where(lane == key_col, live_col, 0), axis=0, keepdims=True)
    counts_col = jnp.sum(jnp.where(iota((lanes, slots), 0) == key_row, live_row, 0), axis=1, keepdims=True)
    steps, steps_col = (counts + 1) >> 1, (counts_col + 1) >> 1
    chosen = (lane < key_col) & (lane >= by_group(key_col, floors))
    base_col = jnp.sum(jnp.where(chosen, steps, 0), axis=1, keepdims=True) + by_group(key_col, starts)
    place = jnp.where(live_col > 0, base_col * 2 + within, -1)
    hit = place == lane
    index = jnp.sum(jnp.where(hit, iota((slots, lanes), 0) - slots, 0), axis=0, keepdims=True) + slots
    other = jnp.sum(jnp.where(hit, other_col, 0), axis=0, keepdims=True)
    opens = (place == lane * 2) & (within == 0)
    carry = 1 - jnp.sum(jnp.where(opens, 1, 0), axis=0, keepdims=True)
    above, below = iota((lanes, lanes), 0), iota((1, lanes), 1)
    upto = (above <= below) & (above >= by_group(below, floors))
    ends = jnp.sum(jnp.where(upto, steps_col, 0), axis=0, keepdims=True) + by_group(below, starts)
    last = jnp.where(counts > 0, ends - 1, empty)
    rows = [index, other, carry, last]
    return jnp.concatenate(rows + [jnp.zeros((1, lanes), jnp.int32)] * (8 - len(rows)), axis=0)


def kernel(
    dims,
    cb_hbm, rb_hbm, count_s, vf_hbm, cf_hbm, coef_hbm,
    cw1_hbm, cbias_hbm, cw2_hbm, cw3_hbm, cgain_hbm, cshift_hbm,
    vw1_hbm, vbias_hbm, vw2_hbm, vw3_hbm, vgain_hbm, vshift_hbm,
    con_out, sums, base, feat, order_out, vw2, vw3, vgain, vshift,
    cb_v, rb_v, cf, cw1, cbias, cw2, cw3, cgain, cshift, vw1, vbias,
    raw, half, scan, paired, part, arrive, window, mixed, conbuf, orderf_v, orderf_s, orderb_v, orderb_s,
    raw_sem, feat_sem, small_sem, weight_sem, order_sem, psend, precv, wsend, wrecv,
):
    nb, nc, slots, size, cols, lanes, groups, steps, pairs = dims
    chunks = sum(groups)
    band = lax.axis_index("band")
    cut = lax.axis_index("cuts")
    has_next = band < nb - 1
    has_prev = band > 0
    width = feat.shape[2]
    cores = 2 if nc % 2 == 0 else 1
    chips = nc // cores
    chip, core = cut // cores, lax.rem(cut, cores)

    def member(far, which):
        return lax.rem(chip + far, chips) * cores + which

    far_first = [member(f, c) for f in range(chips - 1, 0, -1) for c in reversed(range(cores))]
    everyone = far_first + [member(0, c) for c in reversed(range(cores))]
    others = far_first + [member(0, cores - 1 - core)][: cores - 1]

    small = [
        pltpu.make_async_copy(src, dst, small_sem.at[i])
        for i, (src, dst) in enumerate(((cb_hbm, cb_v), (rb_hbm, rb_v)))
    ]
    for copy in small:
        copy.start()

    def raw_copy(i):
        piece = pl.ds(i * CHUNK, CHUNK)
        return pltpu.make_async_copy(coef_hbm.at[piece], raw.at[piece], raw_sem.at[i])

    for i in range(AHEAD):
        raw_copy(i).start()
    feat_copy = pltpu.make_async_copy(vf_hbm, feat, feat_sem)
    feat_copy.start()
    weights = [
        pltpu.make_async_copy(src, dst, weight_sem.at[i])
        for i, (src, dst) in enumerate((
            (cf_hbm, cf), (cw1_hbm, cw1), (cbias_hbm, cbias), (cw2_hbm, cw2), (cw3_hbm, cw3),
            (cgain_hbm, cgain), (cshift_hbm, cshift), (vw1_hbm, vw1), (vbias_hbm, vbias), (vw2_hbm, vw2),
            (vw3_hbm, vw3), (vgain_hbm, vgain), (vshift_hbm, vshift)))
    ]
    barrier = pltpu.get_barrier_semaphore()
    for d in range(1, nc):
        pl.semaphore_signal(barrier, inc=1, device_id=(band, lax.rem(cut + d, nc)), device_id_type=MESH)

    @pl.when(has_next)
    def _():
        for d in range(nc):
            pl.semaphore_signal(barrier, inc=1, device_id=(band + 1, lax.rem(cut + d, nc)), device_id_type=MESH)

    @pl.when(has_prev)
    def _():
        for d in range(nc):
            pl.semaphore_signal(barrier, inc=1, device_id=(band - 1, lax.rem(cut + d, nc)), device_id_type=MESH)

    half[slots] = jnp.zeros((size, size), BF16)
    scan[sum(steps)] = jnp.zeros((size, width), F32)
    sums[pairs] = jnp.zeros(sums.shape[1:], F32)

    @pl.when(jnp.logical_not(has_prev))
    def _():
        arrive[pl.ds(nc, nc)] = jnp.zeros((nc,) + arrive.shape[1:], BF16)

    @pl.when(jnp.logical_not(has_next))
    def _():
        window[pl.ds(nc, nc)] = jnp.zeros((nc,) + window.shape[1:], BF16)

    for copy in small:
        copy.wait()
    row_c = cb_v[...]
    row_r = rb_v[...]
    diagonal = lax.broadcasted_iota(jnp.int32, (slots, slots), 0) == lax.broadcasted_iota(jnp.int32, (slots, slots), 1)
    col_c = jnp.sum(jnp.where(diagonal, row_c, 0), axis=1, keepdims=True)
    col_r = jnp.sum(jnp.where(diagonal, row_r, 0), axis=1, keepdims=True)
    count = count_s[0]
    slot_row = lax.broadcasted_iota(jnp.int32, (1, slots), 1)
    slot_col = lax.broadcasted_iota(jnp.int32, (slots, 1), 0)
    live_row = jnp.where(slot_row < count, 1, 0)
    live_col = jnp.where(slot_col < count, 1, 0)
    blocks = part.shape[1] // size
    keys = 2 * nc * blocks
    bounds = [CHUNK * sum(groups[:g]) for g in range(1, len(groups))]
    starts = tuple(sum(steps[:g]) for g in range(len(groups)))
    late_row = sum(jnp.where(slot_row >= b, keys, 0) for b in bounds)
    late_col = sum(jnp.where(slot_col >= b, keys, 0) for b in bounds)
    orderf_v[...] = order_rows(
        row_r + late_row, col_r + late_col, col_c, live_row, live_col, lanes, keys, starts, sum(steps))
    orderf_copy = pltpu.make_async_copy(orderf_v, orderf_s, order_sem.at[0])
    orderf_copy.start()

    def convert(i):
        raw_copy(i).wait()

        @pl.when(i + AHEAD < chunks)
        def _():
            raw_copy(i + AHEAD).start()

        for u in range(CHUNK):
            half[i * CHUNK + u] = raw[i * CHUNK + u].astype(F32).astype(BF16)

    def convert_step(i, _):
        convert(i)
        return 0

    lax.fori_loop(0, groups[0], convert_step, 0)
    feat_copy.wait()
    orderf_copy.wait()

    carry = jnp.zeros((size, width), F32)
    for g, start in enumerate(starts):
        turns = groups[g + 1] if g + 1 < len(groups) else 1
        chunk = sum(groups[: g + 1])
        unroll = steps[g] // turns

        def forward(k, carry, start=start, unroll=unroll, chunk=chunk, more=g + 1 < len(groups)):
            for u in range(unroll):
                at = start + k * unroll + u
                left = jnp.concatenate([half[orderf_s[0, 2 * at]], half[orderf_s[0, 2 * at + 1]]], axis=1)
                right = jnp.concatenate(
                    [feat[orderf_s[1, 2 * at]], feat[orderf_s[1, 2 * at + 1]]], axis=0)
                term = jnp.dot(left, right, preferred_element_type=F32)
                carry = carry * orderf_s[2, at].astype(F32) + term
                scan[at] = carry
            if more:
                convert(chunk + k)
            return carry

        carry = lax.fori_loop(0, turns, forward, carry)
        if g == 0:
            for copy in weights:
                copy.start()

    def fill(q):
        for e in range(blocks):
            r = q * blocks + e
            total = scan[orderf_s[3, r]]
            for g in range(1, len(groups)):
                total += scan[orderf_s[3, g * keys + r]]
            part[q, e * size : (e + 1) * size] = total.astype(BF16)

    def part_send(i, to, ahead):
        return pltpu.make_async_remote_copy(
            src_ref=part.at[ahead * nc + to], dst_ref=arrive.at[ahead * nc + cut],
            send_sem=psend.at[ahead * nc + i], recv_sem=precv.at[ahead * nc + cut],
            device_id=(band + ahead, to), device_id_type=MESH)

    def part_wait(src, ahead):
        pltpu.make_async_remote_copy(
            src_ref=part.at[0], dst_ref=arrive.at[ahead * nc + src],
            send_sem=psend.at[0], recv_sem=precv.at[ahead * nc + src],
            device_id=(band, cut), device_id_type=MESH).wait_recv()

    for q in range(2 * nc):
        fill(q)

    expected = (nc - 1) + jnp.where(has_next, nc, 0) + jnp.where(has_prev, nc, 0)
    pl.semaphore_wait(barrier, expected)

    @pl.when(has_next)
    def _():
        for i, to in enumerate(everyone):
            part_send(i, to, 1).start()

    for i, to in enumerate(others):
        part_send(i, to, 0).start()

    orderb_v[...] = order_rows(row_c, col_c, col_r, live_row, live_col, lanes, lanes, (0,), pairs)
    orderb_copy = pltpu.make_async_copy(orderb_v, orderb_s, order_sem.at[1])
    orderb_copy.start()
    order_copy = pltpu.make_async_copy(orderb_v, order_out, order_sem.at[2])
    order_copy.start()
    for copy in weights:
        copy.wait()
    orderb_copy.wait()
    order_copy.wait()

    def pair_up(p, _):
        for u in range(PAIR):
            k = p * PAIR + u
            paired[k, :, :size] = half[orderb_s[0, 2 * k]].T
            paired[k, :, size:] = half[orderb_s[0, 2 * k + 1]].T
        return 0

    lax.fori_loop(0, pairs // PAIR, pair_up, 0)

    total = part[cut].astype(F32)
    for d in range(1, nc):
        src = lax.rem(cut + d, nc)
        part_wait(src, 0)
        total += arrive[src].astype(F32)

    @pl.when(has_prev)
    def _():
        for src in range(nc):
            part_wait(src, 1)

    for src in range(nc):
        total += arrive[nc + src].astype(F32)

    con_new = node_update(
        cf[...], total * (1.0 / math.sqrt(size * slots)), cw1[...], cbias[...], cw2[...], cw3[...], cgain[...], cshift[...])
    conbuf[...] = con_new
    window[cut] = con_new

    def win_send(i, to, back):
        return pltpu.make_async_remote_copy(
            src_ref=conbuf, dst_ref=window.at[back * nc + cut],
            send_sem=wsend.at[back * nc + i], recv_sem=wrecv.at[back * nc + cut],
            device_id=(band - back, to), device_id_type=MESH)

    def win_wait(src, back):
        pltpu.make_async_remote_copy(
            src_ref=conbuf, dst_ref=window.at[back * nc + src],
            send_sem=wsend.at[0], recv_sem=wrecv.at[back * nc + src],
            device_id=(band, cut), device_id_type=MESH).wait_recv()

    @pl.when(has_prev)
    def _():
        for i, to in enumerate(everyone):
            win_send(i, to, 1).start()

    for i, to in enumerate(others):
        win_send(i, to, 0).start()

    con_out[...] = con_new

    def base_step(i, _):
        for u in range(BASE):
            c = i * BASE + u
            base[c] = jnp.dot(feat[c], vw1[:width], preferred_element_type=F32) + vbias[...]
        return 0

    lax.fori_loop(0, cols // BASE, base_step, 0)

    def mix(q):
        for e in range(blocks):
            product = jnp.dot(window[q, e * size : (e + 1) * size], vw1[width:], preferred_element_type=F32)
            mixed[q * blocks + e] = (product * (1.0 / math.sqrt(4 * size))).astype(BF16)

    for d in range(1, nc):
        win_wait(lax.rem(cut + d, nc), 0)
    for q in range(nc):
        mix(q)

    @pl.when(has_next)
    def _():
        for src in range(nc):
            win_wait(src, 1)

    for q in range(nc, 2 * nc):
        mix(q)

    def back(k, carry):
        for u in range(BACK):
            at = k * BACK + u
            right = jnp.concatenate([mixed[orderb_s[1, 2 * at]], mixed[orderb_s[1, 2 * at + 1]]], axis=0)
            term = jnp.dot(paired[at], right, preferred_element_type=F32)
            carry = carry * orderb_s[2, at].astype(F32) + term
            sums[at] = carry
        return carry

    lax.fori_loop(0, pairs // BACK, back, jnp.zeros(sums.shape[1:], F32))

    @pl.when(has_next)
    def _():
        for i, to in enumerate(everyone):
            part_send(i, to, 1).wait_send()

    @pl.when(has_prev)
    def _():
        for i, to in enumerate(everyone):
            win_send(i, to, 1).wait_send()

    for i, to in enumerate(others):
        part_send(i, to, 0).wait_send()
        win_send(i, to, 0).wait_send()


def column_kernel(
    size, con, sums, base, feat, order_s, vw2, vw3, vgain, vshift, con_out, var_out,
    result, hidden, middle, output, out_sem, con_sem,
):
    con_copy = pltpu.make_async_copy(con, con_out, con_sem)
    con_copy.start()
    per = TILE // size
    tiles = feat.shape[0] // per
    piece = lambda i: pl.ds(i * TILE, TILE)

    def out_copy(i):
        return pltpu.make_async_copy(result.at[piece(i)], var_out.at[piece(i)], out_sem.at[i])

    def first(i):
        for e in range(per):
            c = i * per + e
            total = sums[order_s[3, c]] + base[c]
            hidden[i % 2, e * size : (e + 1) * size] = jnp.maximum(total, 0.0).astype(BF16)

    def second(i):
        sums = jnp.dot(hidden[i % 2], vw2[...], preferred_element_type=F32)
        middle[i % 2] = jnp.maximum(sums, 0.0).astype(BF16)

    def third(i):
        sums = jnp.dot(middle[i % 2], vw3[...], preferred_element_type=F32)
        output[i % 2] = feat[i * per : (i + 1) * per].reshape(sums.shape).astype(F32) + sums

    def norm(i):
        result[piece(i)] = layer_norm(output[i % 2], vgain[...], vshift[...]).astype(BF16)
        out_copy(i).start()

    stages = (norm, 3), (third, 2), (second, 1), (first, 0)
    for t in range(tiles + len(stages) - 1):
        for stage, delay in stages:
            if 0 <= t - delay < tiles:
                stage(t - delay)

    con_copy.wait()
    for i in range(tiles):
        out_copy(i).wait()


def on_device(
    nb, nc,
    var_feat, con_feat, slot_column_block, slot_constraint_block, block_count, incidence_coefficients,
    con_first, con_bias, con_second, con_third, con_gain, con_shift,
    var_first, var_bias, var_second, var_third, var_gain, var_shift,
):
    width = var_feat.shape[1]
    slots = slot_column_block.shape[0]
    size = incidence_coefficients.shape[1]
    cols = var_feat.shape[0] // size
    rows = con_feat.shape[0]
    rblocks = 2 * nc * (rows // size)
    chunks = slots // CHUNK
    tail = chunks // 5
    groups = (chunks - 2 * (chunks - tail) // 4 - tail, 2 * (chunks - tail) // 4, tail)
    turns = groups[1:] + (1,)
    steps = tuple(-(-(g * CHUNK + rblocks) // (2 * t)) * t for g, t in zip(groups, turns))
    pairs = -(-(slots + cols) // (2 * BACK)) * BACK
    lanes = -(-max(2 * pairs, 2 * sum(steps), 3 * rblocks) // 128) * 128
    dims = (nb, nc, slots, size, cols, lanes, groups, steps, pairs)
    vmem = pl.BlockSpec(memory_space=pltpu.VMEM)
    smem = pl.BlockSpec(memory_space=pltpu.SMEM)
    hbm = pl.BlockSpec(memory_space=pl.ANY)
    row = lambda v: v.reshape(1, -1)
    con_weights = (con_first, row(con_bias), con_second, con_third, row(con_gain), row(con_shift))
    var_weights = (var_first, row(var_bias), var_second, var_third, row(var_gain), row(var_shift))
    held = lambda v: pltpu.with_memory_space_constraint(v, pltpu.HBM)
    like = lambda v: pltpu.VMEM(v.shape, v.dtype)
    hid = var_first.shape[1]
    handed = pl.pallas_call(
        functools.partial(kernel, dims),
        out_shape=(
            like(con_feat),
            pltpu.VMEM((pairs + 1, size, hid), F32),
            pltpu.VMEM((cols, size, hid), F32),
            pltpu.VMEM((cols, size, width), BF16),
            pltpu.SMEM((8, lanes), jnp.int32),
            *(like(w) for w in var_weights[2:]),
        ),
        in_specs=[hbm] * 2 + [smem] + [hbm] * 15,
        out_specs=(vmem,) * 4 + (smem,) + (vmem,) * 4,
        scratch_shapes=[
            pltpu.VMEM((1, slots), jnp.int32),
            pltpu.VMEM((1, slots), jnp.int32),
            like(con_feat),
            *(like(w) for w in con_weights + var_weights[:2]),
            pltpu.VMEM((slots, size, size), jnp.int32),
            pltpu.VMEM((slots + 1, size, size), BF16),
            pltpu.VMEM((sum(steps) + 1, size, width), F32),
            pltpu.VMEM((pairs, size, 2 * size), BF16),
            pltpu.VMEM((2 * nc, rows, width), BF16),
            pltpu.VMEM((2 * nc, rows, width), BF16),
            pltpu.VMEM((2 * nc, rows, width), BF16),
            pltpu.VMEM((rblocks, size, hid), BF16),
            pltpu.VMEM((rows, width), BF16),
            pltpu.VMEM((8, lanes), jnp.int32),
            pltpu.SMEM((8, lanes), jnp.int32),
            pltpu.VMEM((8, lanes), jnp.int32),
            pltpu.SMEM((8, lanes), jnp.int32),
            pltpu.SemaphoreType.DMA((chunks,)),
            pltpu.SemaphoreType.DMA,
            pltpu.SemaphoreType.DMA((2,)),
            pltpu.SemaphoreType.DMA((13,)),
            pltpu.SemaphoreType.DMA((3,)),
            pltpu.SemaphoreType.DMA((2 * nc,)),
            pltpu.SemaphoreType.DMA((2 * nc,)),
            pltpu.SemaphoreType.DMA((2 * nc,)),
            pltpu.SemaphoreType.DMA((2 * nc,)),
        ],
        compiler_params=pltpu.CompilerParams(
            collective_id=0, has_side_effects=True, vmem_limit_bytes=37 * 1024 * 1024),
        name="layer",
    )(
        *map(held, (row(slot_column_block), row(slot_constraint_block))), block_count,
        *map(held, (var_feat.reshape(cols, size, width), con_feat, incidence_coefficients, *con_weights, *var_weights)),
    )
    spaces = (pltpu.VMEM,) * 4 + (pltpu.SMEM,) + (pltpu.VMEM,) * 4
    return pl.pallas_call(
        functools.partial(column_kernel, size),
        out_shape=(
            jax.ShapeDtypeStruct(con_feat.shape, BF16),
            jax.ShapeDtypeStruct(var_feat.shape, BF16),
        ),
        in_specs=[vmem] * 4 + [smem] + [vmem] * 4,
        out_specs=(hbm, hbm),
        scratch_shapes=[
            pltpu.VMEM(var_feat.shape, BF16),
            pltpu.VMEM((2, TILE, hid), BF16),
            pltpu.VMEM((2, TILE, var_second.shape[1]), BF16),
            pltpu.VMEM((2, TILE, width), F32),
            pltpu.SemaphoreType.DMA((var_feat.shape[0] // TILE,)),
            pltpu.SemaphoreType.DMA,
        ],
        compiler_params=pltpu.CompilerParams(vmem_limit_bytes=8 * 1024 * 1024),
        name="columns",
    )(*map(pltpu.with_memory_space_constraint, handed, spaces))


def solution(mesh):
    both = P(("band", "cuts"))
    wide = P(("band", "cuts"), None)
    in_specs = (wide, wide, both, both, both, P(("band", "cuts"), None, None)) + (P(),) * 12
    body = functools.partial(on_device, mesh.shape["band"], mesh.shape["cuts"])
    return jax.shard_map(body, mesh=mesh, in_specs=in_specs, out_specs=(wide, wide), check_vma=False)
```

time: 25.6 us -> 25.6 us (level)
  no operation moved by 1% of the time
where the time goes in v2:
time: 25.6 us; the launch traced here: 25.5 us
  Pallas kernels  24.2 us (95%)
  between operations  1.29 us (5%)
    pallas_call x1, Pallas kernels, on_device(): pl.pallas_call(functools.partial(kernel, dims), out_shape=(like(con_feat)...  21.4 us
    pallas_call x1, Pallas kernels, on_device(): pl.pallas_call(functools.partial(column_kernel, size), out_shape=(jax.Sha...  2.76 us

profile of v2, /device:TPU:0, one launch (start us, length us, event | category | flops | bytes accessed | tf_op | source)
XLA Modules:
  0.0 25.5 jit_solution(11638878564791594828)
XLA Ops:
  1.3 21.4 %layer.1 = (bf16[128,128]{1,0:T(8,128)(2,1)S(1)}, f32[101,128,256]{2,1,0:T(8,128)S(1)}, f32[40,128,256]{2,1,0:T(8,128)S(1)}, bf16[40,128,128]{2,1,0:T(8,128)(2,1...) custom-call(s32[1,160]{1,0:T(1,128)} %bitcast.10, ...), custom_call_target="tpu_custom_call" | custom-call | tf_op jit(solution)/shard_map/layer/pallas_call | solution.py:429
  22.7 2.8 %columns.1 = (bf16[128,128]{1,0:T(8,128)(2,1)}, bf16[5120,128]{1,0:T(8,128)(2,1)}) custom-call(bf16[128,128]{1,0:T(8,128)(2,1)S(1)} %get-tuple-element.11.con, f32[101,128,256]{2,1,0:T(8,128)S(1)} %get-tuple-element.12.sums, f32[40,128,256]{2,1,0:T(8,128)S(1)} %get-tuple-element.13.base, bf16[40,128,128]{2,1,0:T(8,128)(2,1)S(1)} %get-tuple-element.14.feat, ...), custom_call_target="tpu_custom_call" | custom-call | tf_op jit(solution)/shard_map/columns/pallas_call | solution.py:477

commit v3 on v2

--- a/solution.py
+++ b/solution.py
@@ -14,13 +14,17 @@
 MESH = pl.DeviceIdType.MESH
 CHUNK = 16
 UNROLL = 8
-BACK = 50
+BACK = 100
 PAIR = 5
 BASE = 4
 AHEAD = 4
 TILE = 512
 
 
+def relu(values):
+    return jnp.maximum(values.astype(BF16), jnp.zeros((), BF16))
+
+
 def layer_norm(values, gain, offset):
     center = values - jnp.mean(values, axis=-1, keepdims=True)
     spread = jnp.mean(center * center, axis=-1, keepdims=True)
@@ -29,8 +33,8 @@
 
 def node_update(feats, scaled_agg, w_first, bias, w_second, w_third, gain, offset):
     joined = jnp.concatenate([feats, scaled_agg.astype(BF16)], axis=1)
-    hidden = jnp.maximum(jnp.dot(joined, w_first, preferred_element_type=F32) + bias, 0.0).astype(BF16)
-    middle = jnp.maximum(jnp.dot(hidden, w_second, preferred_element_type=F32), 0.0).astype(BF16)
+    hidden = relu(jnp.dot(joined, w_first, preferred_element_type=F32) + bias)
+    middle = relu(jnp.dot(hidden, w_second, preferred_element_type=F32))
     output = jnp.dot(middle, w_third, preferred_element_type=F32)
     return layer_norm(feats.astype(F32) + output, gain, offset).astype(BF16)
 
@@ -205,7 +209,7 @@
             return carry
 
         carry = lax.fori_loop(0, turns, forward, carry)
-        if g == 0:
+        if g == len(groups) - 2:
             for copy in weights:
                 copy.start()
 
@@ -293,13 +297,13 @@
             send_sem=wsend.at[0], recv_sem=wrecv.at[back * nc + src],
             device_id=(band, cut), device_id_type=MESH).wait_recv()
 
+    for i, to in enumerate(others):
+        win_send(i, to, 0).start()
+
     @pl.when(has_prev)
     def _():
         for i, to in enumerate(everyone):
             win_send(i, to, 1).start()
-
-    for i, to in enumerate(others):
-        win_send(i, to, 0).start()
 
     con_out[...] = con_new
 
@@ -372,11 +376,11 @@
         for e in range(per):
             c = i * per + e
             total = sums[order_s[3, c]] + base[c]
-            hidden[i % 2, e * size : (e + 1) * size] = jnp.maximum(total, 0.0).astype(BF16)
+            hidden[i % 2, e * size : (e + 1) * size] = relu(total)
 
     def second(i):
         sums = jnp.dot(hidden[i % 2], vw2[...], preferred_element_type=F32)
-        middle[i % 2] = jnp.maximum(sums, 0.0).astype(BF16)
+        middle[i % 2] = relu(sums)
 
     def third(i):
         sums = jnp.dot(middle[i % 2], vw3[...], preferred_element_type=F32)

time: 25.6 us -> 25.1 us (0.980)
  Pallas kernels: 24.2 us -> 23.6 us
    pallas_call x1, Pallas kernels: 21.4 us -> 21 us  [on_device(): pl.pallas_call(functools.partial(kernel, dims), out_shape=(like(con_feat)...]
where the time goes in v3:
time: 25.1 us; the launch traced here: 24.9 us
  Pallas kernels  23.6 us (94%)
  between operations  1.29 us (5%)
    pallas_call x1, Pallas kernels, on_device(): pl.pallas_call(functools.partial(kernel, dims), out_shape=(like(con_feat)...  21 us
    pallas_call x1, Pallas kernels, on_device(): pl.pallas_call(functools.partial(column_kernel, size), out_shape=(jax.Sha...  2.65 us

profile of v3, /device:TPU:0, one launch (start us, length us, event | category | flops | bytes accessed | tf_op | source)
XLA Modules:
  0.0 24.9 jit_solution(17403978965816268936)
XLA Ops:
  1.3 21.0 %layer.1 = (bf16[128,128]{1,0:T(8,128)(2,1)S(1)}, f32[101,128,256]{2,1,0:T(8,128)S(1)}, f32[40,128,256]{2,1,0:T(8,128)S(1)}, bf16[40,128,128]{2,1,0:T(8,128)(2,1...) custom-call(s32[1,160]{1,0:T(1,128)} %bitcast.10, ...), custom_call_target="tpu_custom_call" | custom-call | tf_op jit(solution)/shard_map/layer/pallas_call | solution.py:433
  22.3 2.6 %columns.1 = (bf16[128,128]{1,0:T(8,128)(2,1)}, bf16[5120,128]{1,0:T(8,128)(2,1)}) custom-call(bf16[128,128]{1,0:T(8,128)(2,1)S(1)} %get-tuple-element.11.con, f32[101,128,256]{2,1,0:T(8,128)S(1)} %get-tuple-element.12.sums, f32[40,128,256]{2,1,0:T(8,128)S(1)} %get-tuple-element.13.base, bf16[40,128,128]{2,1,0:T(8,128)(2,1)S(1)} %get-tuple-element.14.feat, ...), custom_call_target="tpu_custom_call" | custom-call | tf_op jit(solution)/shard_map/columns/pallas_call | solution.py:481

commit v4 on v3

--- a/solution.py
+++ b/solution.py
@@ -80,7 +80,7 @@
     con_out, sums, base, feat, order_out, vw2, vw3, vgain, vshift,
     cb_v, rb_v, cf, cw1, cbias, cw2, cw3, cgain, cshift, vw1, vbias,
     raw, half, scan, paired, part, arrive, window, mixed, conbuf, orderf_v, orderf_s, orderb_v, orderb_s,
-    raw_sem, feat_sem, small_sem, weight_sem, order_sem, psend, precv, wsend, wrecv,
+    raw_sem, feat_sem, small_sem, weight_sem, order_sem, psend, precv, wsend, wrecv, rsend,
 ):
     nb, nc, slots, size, cols, lanes, groups, steps, pairs = dims
     chunks = sum(groups)
@@ -297,13 +297,25 @@
             send_sem=wsend.at[0], recv_sem=wrecv.at[back * nc + src],
             device_id=(band, cut), device_id_type=MESH).wait_recv()
 
-    for i, to in enumerate(others):
+    peer = member(0, cores - 1 - core)
+    cross = [member(f, cores - 1 - core) for f in range(chips - 1, 0, -1)]
+    rest = [member(f, core) for f in range(chips - 1, 0, -1)]
+    ahead = cross + [peer]
+
+    def relay(src, back):
+        slot = back * nc + src
+        return pltpu.make_async_remote_copy(
+            src_ref=window.at[slot], dst_ref=window.at[slot],
+            send_sem=rsend.at[slot], recv_sem=wrecv.at[slot],
+            device_id=(band, peer), device_id_type=MESH)
+
+    @pl.when(has_prev)
+    def _():
+        for i, to in enumerate(ahead):
+            win_send(i, to, 1).start()
+
+    for i, to in enumerate(cross + [peer]):
         win_send(i, to, 0).start()
-
-    @pl.when(has_prev)
-    def _():
-        for i, to in enumerate(everyone):
-            win_send(i, to, 1).start()
 
     con_out[...] = con_new
 
@@ -320,14 +332,24 @@
             product = jnp.dot(window[q, e * size : (e + 1) * size], vw1[width:], preferred_element_type=F32)
             mixed[q * blocks + e] = (product * (1.0 / math.sqrt(4 * size))).astype(BF16)
 
-    for d in range(1, nc):
-        win_wait(lax.rem(cut + d, nc), 0)
+    for src in cross:
+        win_wait(src, 0)
+        relay(src, 0).start()
+
+    @pl.when(has_next)
+    def _():
+        for src in reversed(ahead):
+            win_wait(src, 1)
+            relay(src, 1).start()
+
+    for src in [peer] + rest:
+        win_wait(src, 0)
     for q in range(nc):
         mix(q)
 
     @pl.when(has_next)
     def _():
-        for src in range(nc):
+        for src in [cut] + rest:
             win_wait(src, 1)
 
     for q in range(nc, 2 * nc):
@@ -351,12 +373,20 @@
 
     @pl.when(has_prev)
     def _():
-        for i, to in enumerate(everyone):
+        for i, to in enumerate(ahead):
             win_send(i, to, 1).wait_send()
 
     for i, to in enumerate(others):
         part_send(i, to, 0).wait_send()
+    for i, to in enumerate(cross + [peer]):
         win_send(i, to, 0).wait_send()
+    for src in cross:
+        relay(src, 0).wait_send()
+
+    @pl.when(has_next)
+    def _():
+        for src in ahead:
+            relay(src, 1).wait_send()
 
 
 def column_kernel(
@@ -469,6 +499,7 @@
             pltpu.SemaphoreType.DMA((2 * nc,)),
             pltpu.SemaphoreType.DMA((2 * nc,)),
             pltpu.SemaphoreType.DMA((2 * nc,)),
+            pltpu.SemaphoreType.DMA((2 * nc,)),
         ],
         compiler_params=pltpu.CompilerParams(
             collective_id=0, has_side_effects=True, vmem_limit_bytes=37 * 1024 * 1024),

time: 25.1 us -> 24.7 us (0.984)
  Pallas kernels: 23.6 us -> 23.2 us
    pallas_call x1, Pallas kernels: 21 us -> 20.6 us  [on_device(): pl.pallas_call(functools.partial(kernel, dims), out_shape=(like(con_feat)...]
where the time goes in v4:
time: 24.7 us; the launch traced here: 24.5 us
  Pallas kernels  23.2 us (94%)
  between operations  1.29 us (5%)
    pallas_call x1, Pallas kernels, on_device(): pl.pallas_call(functools.partial(kernel, dims), out_shape=(like(con_feat)...  20.6 us
    pallas_call x1, Pallas kernels, on_device(): pl.pallas_call(functools.partial(column_kernel, size), out_shape=(jax.Sha...  2.65 us

profile of v4, /device:TPU:0, one launch (start us, length us, event | category | flops | bytes accessed | tf_op | source)
XLA Modules:
  0.0 24.5 jit_solution(9565719247252520747)
XLA Ops:
  1.3 20.6 %layer.1 = (bf16[128,128]{1,0:T(8,128)(2,1)S(1)}, f32[101,128,256]{2,1,0:T(8,128)S(1)}, f32[40,128,256]{2,1,0:T(8,128)S(1)}, bf16[40,128,128]{2,1,0:T(8,128)(2,1...) custom-call(s32[1,160]{1,0:T(1,128)} %bitcast.10, ...), custom_call_target="tpu_custom_call" | custom-call | tf_op jit(solution)/shard_map/layer/pallas_call | solution.py:463
  21.9 2.6 %columns.1 = (bf16[128,128]{1,0:T(8,128)(2,1)}, bf16[5120,128]{1,0:T(8,128)(2,1)}) custom-call(bf16[128,128]{1,0:T(8,128)(2,1)S(1)} %get-tuple-element.11.con, f32[101,128,256]{2,1,0:T(8,128)S(1)} %get-tuple-element.12.sums, f32[40,128,256]{2,1,0:T(8,128)S(1)} %get-tuple-element.13.base, bf16[40,128,128]{2,1,0:T(8,128)(2,1)S(1)} %get-tuple-element.14.feat, ...), custom_call_target="tpu_custom_call" | custom-call | tf_op jit(solution)/shard_map/columns/pallas_call | solution.py:512

commit v5 on v4

--- a/solution.py
+++ b/solution.py
@@ -342,6 +342,21 @@
             win_wait(src, 1)
             relay(src, 1).start()
 
+    @pl.when(has_next)
+    def _():
+        for i, to in enumerate(everyone):
+            part_send(i, to, 1).wait_send()
+
+    @pl.when(has_prev)
+    def _():
+        for i, to in enumerate(ahead):
+            win_send(i, to, 1).wait_send()
+
+    for i, to in enumerate(others):
+        part_send(i, to, 0).wait_send()
+    for i, to in enumerate(cross + [peer]):
+        win_send(i, to, 0).wait_send()
+
     for src in [peer] + rest:
         win_wait(src, 0)
     for q in range(nc):
@@ -366,20 +381,6 @@
 
     lax.fori_loop(0, pairs // BACK, back, jnp.zeros(sums.shape[1:], F32))
 
-    @pl.when(has_next)
-    def _():
-        for i, to in enumerate(everyone):
-            part_send(i, to, 1).wait_send()
-
-    @pl.when(has_prev)
-    def _():
-        for i, to in enumerate(ahead):
-            win_send(i, to, 1).wait_send()
-
-    for i, to in enumerate(others):
-        part_send(i, to, 0).wait_send()
-    for i, to in enumerate(cross + [peer]):
-        win_send(i, to, 0).wait_send()
     for src in cross:
         relay(src, 0).wait_send()
 

time: 24.7 us -> 24.7 us (level)
  no operation moved by 1% of the time
where the time goes in v5:
time: 24.7 us; the launch traced here: 24.5 us
  Pallas kernels  23.2 us (94%)
  between operations  1.29 us (5%)
    pallas_call x1, Pallas kernels, on_device(): pl.pallas_call(functools.partial(kernel, dims), out_shape=(like(con_feat)...  20.6 us
    pallas_call x1, Pallas kernels, on_device(): pl.pallas_call(functools.partial(column_kernel, size), out_shape=(jax.Sha...  2.65 us

profile of v5, /device:TPU:0, one launch (start us, length us, event | category | flops | bytes accessed | tf_op | source)
XLA Modules:
  0.0 24.5 jit_solution(3547863228961268081)
XLA Ops:
  1.3 20.6 %layer.1 = (bf16[128,128]{1,0:T(8,128)(2,1)S(1)}, f32[101,128,256]{2,1,0:T(8,128)S(1)}, f32[40,128,256]{2,1,0:T(8,128)S(1)}, bf16[40,128,128]{2,1,0:T(8,128)(2,1...) custom-call(s32[1,160]{1,0:T(1,128)} %bitcast.10, ...), custom_call_target="tpu_custom_call" | custom-call | tf_op jit(solution)/shard_map/layer/pallas_call | solution.py:464
  21.9 2.6 %columns.1 = (bf16[128,128]{1,0:T(8,128)(2,1)}, bf16[5120,128]{1,0:T(8,128)(2,1)}) custom-call(bf16[128,128]{1,0:T(8,128)(2,1)S(1)} %get-tuple-element.11.con, f32[101,128,256]{2,1,0:T(8,128)S(1)} %get-tuple-element.12.sums, f32[40,128,256]{2,1,0:T(8,128)S(1)} %get-tuple-element.13.base, bf16[40,128,128]{2,1,0:T(8,128)(2,1)S(1)} %get-tuple-element.14.feat, ...), custom_call_target="tpu_custom_call" | custom-call | tf_op jit(solution)/shard_map/columns/pallas_call | solution.py:513
